TPU v7x, 128 devices: a whole 4x4x4 slice. The times are simulated.
128 devices in a mesh: heads: 8 (over z, core), width: 4 (over y), sae: 4 (over x).
Axes of the slice: x: 4, y: 4, z: 4, core: 2. Of those that a mesh axis runs over, the one named last changes fastest.
Arguments:
- x_in: bfloat16 [512, 4608], P(None, 'width'), may hold values from -64 to 64
- doc_lengths: int32 [4], replicated, may hold values from 1 to 256, 512 in all
- attn_gain: float32 [4608], P('width'), may hold values from 0.25 to 1.75
- w_query: bfloat16 [4608, 4096], P('width', 'heads'), may hold values from -0.09375 to 0.09375
- w_key: bfloat16 [4608, 2048], P('width', 'heads'), may hold values from -0.09375 to 0.09375
- w_value: bfloat16 [4608, 2048], P('width', 'heads'), may hold values from -0.09375 to 0.09375
- w_out: bfloat16 [4096, 4608], P('heads', 'width'), may hold values from -0.09375 to 0.09375
- post_gain: float32 [4608], replicated, may hold values from 0.25 to 1.75
- enc_weight: bfloat16 [4608, 65536], P(None, ('heads', 'width', 'sae')), may hold values from -0.09375 to 0.09375
- enc_bias: float32 [65536], P(('heads', 'width', 'sae')), may hold values from -1.5 to 0.5
- dec_weight: bfloat16 [65536, 4608], P(('heads', 'width', 'sae')), may hold values from -1 to 1
- dec_bias: float32 [4608], replicated, may hold values from -5 to 5
Outputs:
- grad_enc: bfloat16 [4608, 65536], P(None, ('heads', 'width', 'sae'))
- grad_dec: bfloat16 [65536, 4608], P(('heads', 'width', 'sae'))
- total_loss: float32 [], replicated
Inputs may be any that keep to these rules, and one draw needn't show every extreme that they name: `doc_lengths`: lengths of the 4 documents packed in order; they sum to 512.
All inputs are finite; a program needn't handle non-finite values.
Results may differ from a plain program's by a relative error of at most 0.02.
Values may be sent and summed in bfloat16 or wider, within the bound.
A program may use at most 128 MiB of HBM per device.

v0:
```python
import jax
import jax.numpy as jnp
from jax import lax
from jax.sharding import PartitionSpec as P

D = 4608
HEADS = 32
HEAD_DIM = 128
norm_eps = 1e-06
soft_cap = 50.0
rope_base = 10000.0
l1_weight = 3.0


def rotary(values, position):
    half_dim = values.shape[-1] // 2
    frequency = rope_base ** (-2.0 * jnp.arange(half_dim, dtype=jnp.float32) / values.shape[-1])
    angles = position.astype(jnp.float32)[:, None] * frequency[None, :]
    cosine_table = jnp.cos(angles)[:, None, :]
    sine_table = jnp.sin(angles)[:, None, :]
    first_half = values[..., :half_dim]
    second_half = values[..., half_dim:]
    return jnp.concatenate(
        [
            first_half * cosine_table - second_half * sine_table,
            second_half * cosine_table + first_half * sine_table,
        ],
        axis=-1,
    )


def attend_rows(query_rows, key_rows, value_rows, allowed_rows, scale):
    scores = (
        jnp.einsum("tkgd,skd->kgts", query_rows, key_rows, preferred_element_type=jnp.float32)
        * scale
    )
    capped = soft_cap * jnp.tanh(scores / soft_cap)
    weights = jnp.where(allowed_rows[None, None], jnp.exp(capped), 0.0)
    totals = jnp.sum(weights, axis=-1, keepdims=True)
    probs_bf = (weights / totals).astype(jnp.bfloat16)
    return jnp.einsum(
        "kgts,skd->tkgd", probs_bf, value_rows, preferred_element_type=jnp.float32
    ).astype(jnp.bfloat16)


def per_device(
    x_in,
    doc_lengths,
    attn_gain,
    w_query,
    w_key,
    w_value,
    w_out,
    post_gain,
    enc_weight,
    enc_bias,
    dec_weight,
    dec_bias,
):
    tokens = x_in.shape[0]
    query_heads = w_query.shape[1] // HEAD_DIM
    value_heads = w_key.shape[1] // HEAD_DIM
    boundary = jnp.cumsum(doc_lengths)
    position = jnp.arange(tokens, dtype=jnp.int32)
    segment = jnp.sum((boundary[None, :] <= position[:, None]).astype(jnp.int32), axis=1)
    allowed = (segment[:, None] == segment[None, :]) & (position[None, :] <= position[:, None])
    x_float = x_in.astype(jnp.float32)
    scaled = (x_float * attn_gain).astype(jnp.bfloat16)
    query_part = jnp.dot(scaled, w_query, preferred_element_type=jnp.float32)
    key_part = jnp.dot(scaled, w_key, preferred_element_type=jnp.float32)
    value_part = jnp.dot(scaled, w_value, preferred_element_type=jnp.float32)
    square_part = jnp.sum(x_float * x_float, axis=1)
    query_raw, key_raw, value_raw, square_sums = lax.psum(
        (query_part, key_part, value_part, square_part), "width"
    )
    inverse_rms = lax.rsqrt(square_sums / D + norm_eps)
    query = rotary(
        (query_raw * inverse_rms[:, None]).reshape(tokens, query_heads, HEAD_DIM), position
    ).astype(jnp.bfloat16)
    key_rows = rotary(
        (key_raw * inverse_rms[:, None]).reshape(tokens, value_heads, HEAD_DIM), position
    ).astype(jnp.bfloat16)
    value_rows = (
        (value_raw * inverse_rms[:, None])
        .reshape(tokens, value_heads, HEAD_DIM)
        .astype(jnp.bfloat16)
    )
    query4 = query.reshape(tokens, value_heads, query_heads // value_heads, HEAD_DIM)
    pieces_out = attend_rows(query4, key_rows, value_rows, allowed, (D // HEADS) ** (-0.5))
    mixed = pieces_out.reshape(tokens, query_heads * HEAD_DIM)
    proj_part = jnp.dot(mixed, w_out, preferred_element_type=jnp.float32)
    attn_sum = lax.psum(proj_part, "heads")
    attn_local = attn_sum.astype(jnp.bfloat16)
    attn_proj, x_full = (
        lax.all_gather(attn_local, "width", axis=1, tiled=True),
        lax.all_gather(x_in, "width", axis=1, tiled=True),
    )
    proj_float = attn_proj.astype(jnp.float32)
    inverse_post = lax.rsqrt(jnp.sum(proj_float * proj_float, axis=1) / D + norm_eps)
    resid = (x_full.astype(jnp.float32) + proj_float * inverse_post[:, None] * post_gain).astype(
        jnp.bfloat16
    )
    centered = (resid.astype(jnp.float32) - dec_bias).astype(jnp.bfloat16)
    pre_acts = jnp.dot(centered, enc_weight, preferred_element_type=jnp.float32) + enc_bias
    latent_acts = jnp.maximum(pre_acts, 0.0).astype(jnp.bfloat16)
    row_norms = jnp.sqrt(jnp.sum(jnp.square(dec_weight.astype(jnp.float32)), axis=1) + norm_eps)
    act_sums = jnp.sum(latent_acts.astype(jnp.float32), axis=0)
    penalty_part = jnp.sum(act_sums * row_norms)
    recon_part = jnp.dot(latent_acts, dec_weight, preferred_element_type=jnp.float32)
    recon = lax.psum(recon_part, ("heads", "width", "sae")) + dec_bias
    error = recon - resid.astype(jnp.float32)
    squares_total = jnp.sum(error * error)
    penalty_total = lax.psum(penalty_part, ("heads", "width", "sae"))
    grad_recon = (2.0 / tokens * error).astype(jnp.bfloat16)
    total_loss = (squares_total + l1_weight * penalty_total) / (tokens * D)
    upstream = lax.dot_general(
        grad_recon, dec_weight, (((1,), (1,)), ((), ())), preferred_element_type=jnp.float32
    )
    grad_pre = jnp.where(pre_acts > 0, upstream + l1_weight * row_norms / tokens, 0.0).astype(
        jnp.bfloat16
    )
    grad_enc = lax.dot_general(
        centered, grad_pre, (((0,), (0,)), ((), ())), preferred_element_type=jnp.float32
    ).astype(jnp.bfloat16)
    decoder_term = lax.dot_general(
        latent_acts, grad_recon, (((0,), (0,)), ((), ())), preferred_element_type=jnp.float32
    )
    grad_dec = (
        decoder_term
        + l1_weight
        / tokens
        * act_sums[:, None]
        * dec_weight.astype(jnp.float32)
        / row_norms[:, None]
    ).astype(jnp.bfloat16)
    return (grad_enc, grad_dec, total_loss)


def solution(mesh):
    placed = (
        P(None, "width"),
        P(),
        P("width"),
        P("width", "heads"),
        P("width", "heads"),
        P("width", "heads"),
        P("heads", "width"),
        P(),
        P(None, ("heads", "width", "sae")),
        P(("heads", "width", "sae")),
        P(("heads", "width", "sae"), None),
        P(),
    )
    return jax.shard_map(
        per_device,
        mesh=mesh,
        in_specs=placed,
        out_specs=(P(None, ("heads", "width", "sae")), P(("heads", "width", "sae"), None), P()),
        check_vma=False,
    )
```

profile of v0, /device:TPU:1, one launch (start us, length us, event | category | flops | bytes accessed | tf_op | source)
XLA Modules:
  0.0 471.6 jit_solution(9375944868353371698)
XLA Ops:
  7.2 0.0 copy-start
  7.2 0.0 copy-start.3
  7.2 0.0 copy-start.11
  7.2 0.0 copy-start.10
  7.2 0.0 copy-start.13
  7.2 0.0 all-reduce.7.cloned.1.call-start
  7.3 3.6 fusion.23
  10.9 2.7 fusion.25
  13.6 0.0 copy-done.3
  13.6 0.0 copy-done.11
  13.6 1.3 fusion.27
  14.9 0.0 all-reduce.7.cloned.1.call-update
  15.0 0.0 all-gather.5.cloned.1.call-start
  15.0 0.2 reduce-window.8
  15.2 0.3 fusion.14
  15.5 9.5 %psum.50 = f32[512]{0:T(512)S(1)} all-reduce(f32[512]{0:T(512)S(1)} %fusion.14), channel_id=1, replica_groups=mesh['heads'=8,'width'=4,'sae'=4] {'width'}, use_global_device_ids=true, to_apply=%region_2.3 | all-reduce | flops 512 | bytes 4096 | tf_op jit(solution)/shard_map/psum | solution.py:73
  25.1 0.1 convert_reduce_fusion.1
  25.2 0.9 fusion.22
  26.1 1.7 multiply_cosine_fusion
  27.8 49.0 %all-reduce.7.cloned.1.call-done = (f32[512,256]{1,0:T(8,128)}, f32[512,512]{1,0:T(8,128)}, f32[512,256]{1,0:T(8,128)}) async-done(((f32[512,256]{1,0:T(8,128)}, f32[512,512]{1,0:T(8,128)}, f32[512,256]{1,0:T(8,128)}), (f32[512,256]{1,0:T(8,128)}, f32[512,512]{1,0:T(8,128)}, f32[512,256]{1,0:T(8,128)})) %all-reduce.7.cloned.1.call-update) | async-done | bytes 2097168 | tf_op jit(solution)/shard_map/psum | solution.py:73
  76.9 2.1 broadcast_multiply_fusion.1
  78.9 0.3 reshape.168
  79.2 1.5 fusion.40
  80.7 1.4 broadcast_multiply_fusion
  82.1 0.4 reshape.169
  82.4 0.0 copy-start.6
  82.4 0.0 copy-start.5
  82.5 1.8 subtract_convert_fusion
  84.3 0.1 copy.23
  84.3 0.1 copy.24
  84.4 0.1 copy.30
  84.6 0.0 copy-done.5
  84.6 1.3 subtract_convert_fusion.1
  85.9 0.0 copy-start.7
  85.9 2.9 fusion.12
  88.8 1.6 fusion.21
  90.4 0.9 fusion.41
  91.3 0.0 copy-start.8
  91.3 52.5 %all-reduce.8 = bf16[512,1152]{1,0:T(8,128)(2,1)} all-reduce(f32[512,1152]{1,0:T(8,128)S(1)} %fusion.41), channel_id=1, replica_groups=mesh['heads'=8,'width'=4,'sae'=4] {'heads'}, use_global_device_ids=true, to_apply=%region_8.9 | all-reduce | flops 589824 | bytes 3538944 | tf_op jit(solution)/shard_map/psum | solution.py:92
  143.8 0.0 all-gather.5.cloned.1.call-update
  143.8 0.0 all-gather.3.cloned.1.call-start
  143.8 0.7 all-gather.3.cloned.1.call-update
  144.5 0.2 all-reduce.5.cloned.1.call-start
  144.8 51.8 %all-gather.5.cloned.1.call-done = bf16[512,4608]{1,0:T(8,128)(2,1)} async-done(((bf16[512,1152]{1,0:T(8,128)(2,1)}), bf16[512,4608]{1,0:T(8,128)(2,1)}) %all-gather.5.cloned.1.call-update) | async-done | bytes 4718608 | tf_op jit(solution)/shard_map/all_gather | solution.py:95
  196.6 3.3 fusion
  199.9 0.0 copy-start.12
  200.0 51.3 %all-gather.3.cloned.1.call-done = bf16[512,4608]{1,0:T(8,128)(2,1)} async-done(((bf16[512,1152]{1,0:T(8,128)(2,1)}), bf16[512,4608]{1,0:T(8,128)(2,1)}) %all-gather.3.cloned.1.call-update) | async-done | bytes 4718608 | tf_op jit(solution)/shard_map/all_gather | solution.py:96
  251.3 0.0 copy-done.8
  251.3 5.9 %fusion.3 = bf16[512,4608]{1,0:T(8,128)(2,1)S(1)} fusion(bf16[512,4608]{1,0:T(8,128)(2,1)} %all-gather.5.cloned.1.call-done, bf16[512,4608]{1,0:T(8,128)(2,1)} %all-gather.3.cloned.1.call-done, f32[4608]{0:T(1024)S(1)} %copy-done.8, f32[512]{0:T(512)S(1)} %add_rsqrt_fusion), kind=kLoop, calls=%fused_computation.9 | loop fusion | flops 14155776 | bytes 14176256 | tf_op jit(solution)/shard_map/convert_element_type | solution.py:100
  257.2 0.0 copy-start.2
  257.2 0.0 slice-start.1
  257.3 6.4 %convert_reduce_fusion = (f32[512]{0:T(512)S(1)}, f32[512,512]{1,0:T(8,128)S(1)}) fusion(f32[512]{0:T(512)S(1)} %copy-done.12, bf16[4608,512]{1,0:T(8,128)(2,1)} %param.20, bf16[512,4608]{1,0:T(8,128)(2,1)S(1)} %fusion.3, f32[4608]{0:T(1024)S(1)} %copy-done.9), kind=kOutput, calls=%fused_computation.32 | convolution fusion | flops 2424045056 | bytes 10508288 | tf_op jit(solution)/shard_map/dot_general | solution.py:104
  263.7 5.1 %fusion.39 = f32[512,4608]{1,0:T(8,128)} fusion(bf16[512,4608]{1,0:T(8,128)(2,1)S(1)} %bitcast.41, f32[512,512]{1,0:T(8,128)S(1)} %get-tuple-element.25), kind=kOutput, calls=%fused_computation.69 | convolution fusion | flops 2416443392 | bytes 15204352 | tf_op jit(solution)/shard_map/dot_general | solution.py:109
  268.8 0.0 all-reduce.5.cloned.1.call-update
  268.8 3.3 fusion.5
  272.2 0.6 multiply_reduce_fusion.1
  272.8 65.8 %psum.55 = f32[]{:T(128)} all-reduce(f32[]{:T(128)} %get-tuple-element.16), channel_id=1, replica_groups=mesh['heads'=8,'width'=4,'sae'=4] {'heads','width','sae'}, use_global_device_ids=true, to_apply=%region_15.16 | all-reduce | flops 1 | bytes 8 | tf_op jit(solution)/shard_map/psum | solution.py:113
  339.2 94.4 %all-reduce.5.cloned.1.call-done = f32[512,4608]{1,0:T(8,128)} async-done(((f32[512,4608]{1,0:T(8,128)}), f32[512,4608]{1,0:T(8,128)}) %all-reduce.5.cloned.1.call-update) | async-done | bytes 9437200 | tf_op jit(solution)/shard_map/psum | solution.py:110
  433.6 8.4 %multiply_reduce_fusion = (f32[]{:T(128)}, bf16[512,4608]{1,0:T(8,128)(2,1)S(1)}) fusion(bf16[512,4608]{1,0:T(8,128)(2,1)} %copy-done.2, f32[512,4608]{1,0:T(8,128)} %all-reduce.5.cloned.1.call-done, f32[4608]{0:T(1024)S(1)} %copy-done.9), kind=kLoop, calls=%fused_computation.15 | loop fusion | flops 16515071 | bytes 18892804 | tf_op jit(solution)/shard_map/reduce_sum | solution.py:112
  442.0 6.7 %fusion.20 = bf16[512,512]{1,0:T(8,128)(2,1)S(1)} fusion(bf16[512,4608]{1,0:T(8,128)(2,1)S(1)} %get-tuple-element.7, bf16[512,4608]{1,0:T(8,128)(2,1)} %param.22, f32[512,512]{1,0:T(8,128)S(1)} %get-tuple-element.25, f32[512]{0:T(512)S(1)} %get-tuple-element.17), kind=kOutput, calls=%fused_computation.30 | convolution fusion | flops 2416967680 | bytes 11012096 | tf_op jit(solution)/shard_map/dot_general | solution.py:116
  448.7 6.8 %convolution_convert_fusion = bf16[4608,512]{1,0:T(8,128)(2,1)} fusion(bf16[512,512]{1,0:T(8,128)(2,1)S(1)} %fusion.20, bf16[512,4608]{1,0:T(8,128)(2,1)} %copy-done.2, f32[4608]{0:T(1024)S(1)} %copy-done.9), kind=kOutput, calls=%fused_computation.17 | convolution fusion | flops 2425356288 | bytes 9979904 | tf_op jit(solution)/shard_map/dot_general | solution.py:122
  456.1 0.0 copy-start.1
  456.1 7.8 %fusion.8 = bf16[512,4608]{1,0:T(8,128)(2,1)} fusion(bf16[512,4608]{1,0:T(8,128)(2,1)} %param.22, bf16[512,4608]{1,0:T(8,128)(2,1)} %copy-done.4, f32[512]{0:T(512)S(1)} %get-tuple-element.18, f32[512]{0:T(512)S(1)} %get-tuple-element.19, f32[512,512]{1,0:T(8,128)S(1)} %get-tuple-element.25), kind=kOutput, calls=%fused_computation.14 | convolution fusion | flops 2428239872 | bytes 15208448 | tf_op jit(solution)/shard_map/dot_general | solution.py:125
  463.9 0.0 copy-done.1
  (19 shorter events, 0.1 us)
Async XLA Ops:
  7.2 83.3 %copy-start = (bf16[512,1152]{1,0:T(8,128)(2,1)S(1)}, bf16[512,1152]{1,0:T(8,128)(2,1)}, u32[]{:S(2)}) copy-start(bf16[512,1152]{1,0:T(8,128)(2,1)} %param.18) | copy-start | bytes 3538948
  7.2 6.5 %copy-start.3 = (bf16[512,1152]{1,0:T(8,128)(2,1)S(1)}, bf16[512,1152]{1,0:T(8,128)(2,1)}, u32[]{:S(2)}) copy-start(bf16[512,1152]{1,0:T(8,128)(2,1)} %param.12) | copy-start | bytes 3538948
  7.2 6.4 %copy-start.11 = (f32[1152]{0:T(1024)S(1)}, f32[1152]{0:T(1024)}, u32[]{:S(2)}) copy-start(f32[1152]{0:T(1024)} %param.14) | copy-start | bytes 13828
  7.2 6.4 %copy-start.10 = (bf16[1152,256]{1,0:T(8,128)(2,1)S(1)}, bf16[1152,256]{1,0:T(8,128)(2,1)}, u32[]{:S(2)}) copy-start(bf16[1152,256]{1,0:T(8,128)(2,1)} %param.17) | copy-start | bytes 1769476
  7.2 7.8 %copy-start.13 = (s32[4]{0:T(128)S(1)}, s32[4]{0:T(128)}, u32[]{:S(2)}) copy-start(s32[4]{0:T(128)} %param.13) | copy-start | bytes 52
  7.2 69.6 %all-reduce.7.cloned.1.call-start = ((), (), s32[]{:S(2)}) async-start(), calls=%async_computation.3 | async-start | bytes 4194304 | tf_op jit(solution)/shard_map/psum | solution.py:73
  15.0 181.6 %all-gather.5.cloned.1.call-start = ((), (), s32[]{:S(2)}) async-start(), calls=%async_computation.1 | async-start | bytes 5898240 | tf_op jit(solution)/shard_map/all_gather | solution.py:95
  82.4 2.0 copy-start.6
  82.4 2.1 copy-start.5
  85.9 2.9 copy-start.7
  91.3 160.0 %copy-start.8 = (f32[4608]{0:T(1024)S(1)}, f32[4608]{0:T(1024)}, u32[]{:S(2)}) copy-start(f32[4608]{0:T(1024)} %param.19) | copy-start | bytes 55300
  143.8 107.5 %all-gather.3.cloned.1.call-start = ((), (), s32[]{:S(2)}) async-start(), calls=%async_computation | async-start | bytes 5898240 | tf_op jit(solution)/shard_map/all_gather | solution.py:96
  144.5 289.1 %all-reduce.5.cloned.1.call-start = ((), (), s32[]{:S(2)}) async-start(), calls=%async_computation.2 | async-start | bytes 18874368 | tf_op jit(solution)/shard_map/psum | solution.py:110
  199.9 57.3 %copy-start.9 = (f32[4608]{0:T(1024)S(1)}, f32[4608]{0:T(1024)}, u32[]{:S(2)}) copy-start(f32[4608]{0:T(1024)} %param.23) | copy-start | bytes 55300
  199.9 57.3 %copy-start.12 = (f32[512]{0:T(512)S(1)}, f32[512]{0:T(512)}, u32[]{:S(2)}) copy-start(f32[512]{0:T(512)} %param.21) | copy-start | bytes 6148
  251.3 12.4 %slice-start = ((s8[4718592]{0:T(1024)(128)(4,1)}), s8[4194304]{0:T(1024)(128)(4,1)S(1)}, s32[]{:S(2)}) async-start(s8[4718592]{0:T(1024)(128)(4,1)} %bitcast.40), calls=%async_computation.4 | async-start | bytes 8388608
  257.2 6.4 %copy-start.2 = (bf16[512,4608]{1,0:T(8,128)(2,1)}, bf16[512,4608]{1,0:T(8,128)(2,1)S(1)}, u32[]{:S(2)}) copy-start(bf16[512,4608]{1,0:T(8,128)(2,1)S(1)} %fusion.3) | copy-start | bytes 14155780
  257.2 6.5 %slice-start.1 = ((s8[4718592]{0:T(1024)(128)(4,1)}), s8[524288]{0:T(1024)(128)(4,1)S(1)}, s32[]{:S(2)}) async-start(s8[4718592]{0:T(1024)(128)(4,1)} %bitcast.40), calls=%async_computation.5 | async-start | bytes 1048576
  442.0 6.7 %copy-start.4 = (bf16[512,4608]{1,0:T(8,128)(2,1)}, bf16[512,4608]{1,0:T(8,128)(2,1)S(1)}, u32[]{:S(2)}) copy-start(bf16[512,4608]{1,0:T(8,128)(2,1)S(1)} %get-tuple-element.7) | copy-start | bytes 14155780
  456.1 7.9 %copy-start.1 = (bf16[512,1152]{1,0:T(8,128)(2,1)S(1)}, bf16[512,1152]{1,0:T(8,128)(2,1)}, u32[]{:S(2)}) copy-start(bf16[512,1152]{1,0:T(8,128)(2,1)} %param.18) | copy-start | bytes 3538948
Sparse Core Ops, SparseCore 0:
  15.1 61.7 all-reduce.6
  143.9 52.6 all-gather.4
  198.3 52.9 all-gather.2
  268.9 164.6 all-reduce.4
where the time goes:
time: 472 us
  waiting for transfers between devices  247 us (52%)
  blocking collectives  128 us (27%)
  matrix products  45.7 us (10%)
  other arithmetic  31.4 us (7%)
  between operations  16.5 us (3%)
    psum x1, waiting for transfers between devices, per_device(): recon = lax.psum(recon_part, ('heads', 'width', 'sae')) + dec_bias  94.4 us
    psum x1, blocking collectives, per_device(): penalty_total = lax.psum(penalty_part, ('heads', 'width', 'sae'))  65.8 us
    psum x1, blocking collectives, per_device(): attn_sum = lax.psum(proj_part, 'heads')  52.5 us
    all_gather x1, waiting for transfers between devices, per_device(): lax.all_gather(attn_local, 'width', axis=1, tiled=True)  51.8 us
    all_gather x1, waiting for transfers between devices, per_device(): lax.all_gather(x_in, 'width', axis=1, tiled=True)  51.3 us
    psum x1, waiting for transfers between devices, per_device(): lax.psum((query_part, key_part, value_part, square_part), 'width')  49 us
    psum x1, blocking collectives, per_device(): lax.psum((query_part, key_part, value_part, square_part), 'width')  9.54 us
  transfers between devices with their start and end apart: 4, of which 4 were waited for; matrix products, arithmetic and copies ran while one was open for 2% of the time, Pallas kernels for 0%

commit v1 on v0

--- a/solution.py
+++ b/solution.py
@@ -89,7 +89,11 @@
     pieces_out = attend_rows(query4, key_rows, value_rows, allowed, (D // HEADS) ** (-0.5))
     mixed = pieces_out.reshape(tokens, query_heads * HEAD_DIM)
     proj_part = jnp.dot(mixed, w_out, preferred_element_type=jnp.float32)
-    attn_sum = lax.psum(proj_part, "heads")
+    attn_sum = proj_part
+    for hop in (1, 2, 4):
+        attn_sum = attn_sum + lax.ppermute(
+            attn_sum, "heads", [(dev, dev ^ hop) for dev in range(8)]
+        )
     attn_local = attn_sum.astype(jnp.bfloat16)
     attn_proj, x_full = (
         lax.all_gather(attn_local, "width", axis=1, tiled=True),

time: 472 us -> 533 us (1.13)
  waiting for transfers between devices: 247 us -> 354 us
  blocking collectives: 128 us -> 75.4 us
    ppermute x0 -> x3, waiting for transfers between devices: none -> 106 us  [per_device(): lax.ppermute(attn_sum, 'heads', [(dev, dev ^ hop) for dev in range(8)])]
    psum x1 -> x0, blocking collectives: 52.5 us -> none  [per_device(): attn_sum = lax.psum(proj_part, 'heads')]
  transfers between devices with their start and end apart: 4 -> 7, of which waited for: 4 -> 7; matrix products, arithmetic and copies ran while one was open for 2% -> 2% of each run, Pallas kernels for 0% -> 0%
where the time goes in v1:
time: 533 us
  waiting for transfers between devices  354 us (66%)
  blocking collectives  75.4 us (14%)
  matrix products  45.7 us (9%)
  other arithmetic  33 us (6%)
  between operations  16.5 us (3%)
  starting transfers between devices  5.56 us (1%)
    ppermute x3, waiting for transfers between devices, per_device(): lax.ppermute(attn_sum, 'heads', [(dev, dev ^ hop) for dev in range(8)])  106 us
    psum x1, waiting for transfers between devices, per_device(): recon = lax.psum(recon_part, ('heads', 'width', 'sae')) + dec_bias  94.4 us
    psum x1, blocking collectives, per_device(): penalty_total = lax.psum(penalty_part, ('heads', 'width', 'sae'))  65.8 us
    all_gather x1, waiting for transfers between devices, per_device(): lax.all_gather(attn_local, 'width', axis=1, tiled=True)  52.8 us
    all_gather x1, waiting for transfers between devices, per_device(): lax.all_gather(x_in, 'width', axis=1, tiled=True)  51.3 us
    psum x1, waiting for transfers between devices, per_device(): lax.psum((query_part, key_part, value_part, square_part), 'width')  49 us
  transfers between devices with their start and end apart: 7, of which 7 were waited for; matrix products, arithmetic and copies ran while one was open for 2% of the time, Pallas kernels for 0%

profile of v1, /device:TPU:1, one launch (start us, length us, event | category | flops | bytes accessed | tf_op | source)
XLA Modules:
  0.0 532.5 jit_solution(4236732112478832288)
XLA Ops:
  7.2 0.0 copy-start
  7.2 0.0 copy-start.3
  7.2 0.0 copy-start.11
  7.2 0.0 copy-start.10
  7.2 0.0 copy-start.13
  7.2 0.0 all-reduce.6.cloned.1.call-start
  7.3 3.6 fusion.21
  10.9 2.7 fusion.23
  13.6 0.0 copy-done.3
  13.6 1.3 fusion.25
  14.9 0.0 all-reduce.6.cloned.1.call-update
  15.0 0.0 all-gather.5.cloned.1.call-start
  15.0 0.2 reduce-window.8
  15.2 0.3 fusion.14
  15.5 9.5 %psum.43 = f32[512]{0:T(512)S(1)} all-reduce(f32[512]{0:T(512)S(1)} %fusion.14), channel_id=1, replica_groups=mesh['heads'=8,'width'=4,'sae'=4] {'width'}, use_global_device_ids=true, to_apply=%region_2.3 | all-reduce | flops 512 | bytes 4096 | tf_op jit(solution)/shard_map/psum | solution.py:73
  25.1 0.1 convert_reduce_fusion.1
  25.2 0.9 fusion.20
  26.1 1.7 multiply_cosine_fusion
  27.8 49.0 %all-reduce.6.cloned.1.call-done = (f32[512,256]{1,0:T(8,128)}, f32[512,512]{1,0:T(8,128)}, f32[512,256]{1,0:T(8,128)}) async-done(((f32[512,256]{1,0:T(8,128)}, f32[512,512]{1,0:T(8,128)}, f32[512,256]{1,0:T(8,128)}), (f32[512,256]{1,0:T(8,128)}, f32[512,512]{1,0:T(8,128)}, f32[512,256]{1,0:T(8,128)})) %all-reduce.6.cloned.1.call-update) | async-done | bytes 2097168 | tf_op jit(solution)/shard_map/psum | solution.py:73
  76.8 2.0 broadcast_multiply_fusion.1
  78.9 0.3 reshape.168
  79.2 1.5 fusion.40
  80.7 1.4 broadcast_multiply_fusion
  82.0 0.4 reshape.169
  82.4 1.8 subtract_convert_fusion
  84.2 0.1 copy.23
  84.3 0.1 copy.24
  84.4 0.1 copy.30
  84.6 1.3 subtract_convert_fusion.1
  85.9 2.9 fusion.12
  88.8 1.6 fusion.19
  90.4 0.9 fusion.41
  91.3 0.9 collective-permute-start
  92.2 4.2 collective-permute-done
  96.4 0.2 add.82
  96.6 1.4 collective-permute-start.1
  98.0 51.2 %collective-permute-done.1 = f32[512,1152]{1,0:T(8,128)S(1)} collective-permute-done((f32[512,1152]{1,0:T(8,128)S(1)}, f32[512,1152]{1,0:T(8,128)S(1)}, u32[]{:S(2)}, u32[]{:S(2)}) %collective-permute-start.1) | collective-permute-done | bytes 2359328 | tf_op jit(solution)/shard_map/ppermute | solution.py:94
  149.1 0.2 add.83
  149.4 2.9 collective-permute-start.2
  152.3 50.2 %collective-permute-done.2 = f32[512,1152]{1,0:T(8,128)S(1)} collective-permute-done((f32[512,1152]{1,0:T(8,128)S(1)}, f32[512,1152]{1,0:T(8,128)S(1)}, u32[]{:S(2)}, u32[]{:S(2)}) %collective-permute-start.2) | collective-permute-done | bytes 2359328 | tf_op jit(solution)/shard_map/ppermute | solution.py:94
  202.5 1.2 add_convert_fusion
  203.8 0.0 all-gather.5.cloned.1.call-update
  203.8 0.0 all-gather.3.cloned.1.call-start
  203.8 0.7 all-gather.3.cloned.1.call-update
  204.5 0.2 all-reduce.4.cloned.1.call-start
  204.7 52.8 %all-gather.5.cloned.1.call-done = bf16[512,4608]{1,0:T(8,128)(2,1)} async-done(((bf16[512,1152]{1,0:T(8,128)(2,1)}), bf16[512,4608]{1,0:T(8,128)(2,1)}) %all-gather.5.cloned.1.call-update) | async-done | bytes 4718608 | tf_op jit(solution)/shard_map/all_gather | solution.py:99
  257.5 3.3 fusion
  260.9 0.0 copy-start.12
  260.9 51.3 %all-gather.3.cloned.1.call-done = bf16[512,4608]{1,0:T(8,128)(2,1)} async-done(((bf16[512,1152]{1,0:T(8,128)(2,1)}), bf16[512,4608]{1,0:T(8,128)(2,1)}) %all-gather.3.cloned.1.call-update) | async-done | bytes 4718608 | tf_op jit(solution)/shard_map/all_gather | solution.py:100
  312.2 5.9 %fusion.3 = bf16[512,4608]{1,0:T(8,128)(2,1)S(1)} fusion(bf16[512,4608]{1,0:T(8,128)(2,1)} %all-gather.5.cloned.1.call-done, bf16[512,4608]{1,0:T(8,128)(2,1)} %all-gather.3.cloned.1.call-done, f32[4608]{0:T(1024)S(1)} %copy-done.8, f32[512]{0:T(512)S(1)} %add_rsqrt_fusion), kind=kLoop, calls=%fused_computation.9 | loop fusion | flops 14155776 | bytes 14176256 | tf_op jit(solution)/shard_map/convert_element_type | solution.py:104
  318.2 0.0 copy-start.2
  318.2 0.0 slice-start.1
  318.2 6.4 %convert_reduce_fusion = (f32[512]{0:T(512)S(1)}, f32[512,512]{1,0:T(8,128)S(1)}) fusion(f32[512]{0:T(512)S(1)} %copy-done.12, bf16[4608,512]{1,0:T(8,128)(2,1)} %param.20, bf16[512,4608]{1,0:T(8,128)(2,1)S(1)} %fusion.3, f32[4608]{0:T(1024)S(1)} %copy-done.9), kind=kOutput, calls=%fused_computation.31 | convolution fusion | flops 2424045056 | bytes 10508288 | tf_op jit(solution)/shard_map/dot_general | solution.py:108
  324.6 5.1 fusion.39
  329.7 0.0 all-reduce.4.cloned.1.call-update
  329.7 3.3 fusion.5
  333.1 0.6 multiply_reduce_fusion.1
  333.7 65.8 %psum.47 = f32[]{:T(128)} all-reduce(f32[]{:T(128)} %get-tuple-element.16), channel_id=1, replica_groups=mesh['heads'=8,'width'=4,'sae'=4] {'heads','width','sae'}, use_global_device_ids=true, to_apply=%region_14.15 | all-reduce | flops 1 | bytes 8 | tf_op jit(solution)/shard_map/psum | solution.py:117
  400.2 94.4 %all-reduce.4.cloned.1.call-done = f32[512,4608]{1,0:T(8,128)} async-done(((f32[512,4608]{1,0:T(8,128)}), f32[512,4608]{1,0:T(8,128)}) %all-reduce.4.cloned.1.call-update) | async-done | bytes 9437200 | tf_op jit(solution)/shard_map/psum | solution.py:114
  494.6 8.4 %multiply_reduce_fusion = (f32[]{:T(128)}, bf16[512,4608]{1,0:T(8,128)(2,1)S(1)}) fusion(bf16[512,4608]{1,0:T(8,128)(2,1)} %copy-done.2, f32[512,4608]{1,0:T(8,128)} %all-reduce.4.cloned.1.call-done, f32[4608]{0:T(1024)S(1)} %copy-done.9), kind=kLoop, calls=%fused_computation.15 | loop fusion | flops 16515071 | bytes 18892804 | tf_op jit(solution)/shard_map/reduce_sum | solution.py:116
  502.9 6.7 %convolution_add_fusion = bf16[512,512]{1,0:T(8,128)(2,1)S(1)} fusion(bf16[512,4608]{1,0:T(8,128)(2,1)S(1)} %get-tuple-element.7, bf16[512,4608]{1,0:T(8,128)(2,1)} %param.22, f32[512]{0:T(512)S(1)} %get-tuple-element.17), kind=kOutput, calls=%fused_computation.29 | convolution fusion | flops 2416443392 | bytes 9963520 | tf_op jit(solution)/shard_map/dot_general | solution.py:120
  509.6 6.8 %convolution_convert_fusion = bf16[4608,512]{1,0:T(8,128)(2,1)} fusion(bf16[512,4608]{1,0:T(8,128)(2,1)} %copy-done.2, f32[4608]{0:T(1024)S(1)} %copy-done.9, bf16[512,512]{1,0:T(8,128)(2,1)S(1)} %convolution_add_fusion, f32[512,512]{1,0:T(8,128)S(1)} %get-tuple-element.25), kind=kOutput, calls=%fused_computation.17 | convolution fusion | flops 2425880576 | bytes 11028480 | tf_op jit(solution)/shard_map/dot_general | solution.py:126
  517.0 0.0 copy-start.1
  517.0 7.8 %fusion.8 = bf16[512,4608]{1,0:T(8,128)(2,1)} fusion(bf16[512,4608]{1,0:T(8,128)(2,1)} %param.22, bf16[512,4608]{1,0:T(8,128)(2,1)} %copy-done.4, f32[512]{0:T(512)S(1)} %get-tuple-element.18, f32[512]{0:T(512)S(1)} %get-tuple-element.19, f32[512,512]{1,0:T(8,128)S(1)} %get-tuple-element.25), kind=kOutput, calls=%fused_computation.14 | convolution fusion | flops 2428239872 | bytes 15208448 | tf_op jit(solution)/shard_map/dot_general | solution.py:129
  (27 shorter events, 0.1 us)
Async XLA Ops:
  7.2 83.2 %copy-start = (bf16[512,1152]{1,0:T(8,128)(2,1)S(1)}, bf16[512,1152]{1,0:T(8,128)(2,1)}, u32[]{:S(2)}) copy-start(bf16[512,1152]{1,0:T(8,128)(2,1)} %param.18) | copy-start | bytes 3538948
  7.2 6.4 %copy-start.3 = (bf16[512,1152]{1,0:T(8,128)(2,1)S(1)}, bf16[512,1152]{1,0:T(8,128)(2,1)}, u32[]{:S(2)}) copy-start(bf16[512,1152]{1,0:T(8,128)(2,1)} %param.12) | copy-start | bytes 3538948
  7.2 6.4 %copy-start.11 = (f32[1152]{0:T(1024)S(1)}, f32[1152]{0:T(1024)}, u32[]{:S(2)}) copy-start(f32[1152]{0:T(1024)} %param.14) | copy-start | bytes 13828
  7.2 6.4 %copy-start.10 = (bf16[1152,256]{1,0:T(8,128)(2,1)S(1)}, bf16[1152,256]{1,0:T(8,128)(2,1)}, u32[]{:S(2)}) copy-start(bf16[1152,256]{1,0:T(8,128)(2,1)} %param.17) | copy-start | bytes 1769476
  7.2 7.8 %copy-start.13 = (s32[4]{0:T(128)S(1)}, s32[4]{0:T(128)}, u32[]{:S(2)}) copy-start(s32[4]{0:T(128)} %param.13) | copy-start | bytes 52
  7.2 69.6 %all-reduce.6.cloned.1.call-start = ((), (), s32[]{:S(2)}) async-start(), calls=%async_computation.3 | async-start | bytes 4194304 | tf_op jit(solution)/shard_map/psum | solution.py:73
  15.0 242.6 %all-gather.5.cloned.1.call-start = ((), (), s32[]{:S(2)}) async-start(), calls=%async_computation.1 | async-start | bytes 5898240 | tf_op jit(solution)/shard_map/all_gather | solution.py:99
  82.4 2.0 copy-start.6
  82.4 2.1 copy-start.5
  85.9 2.9 copy-start.7
  91.3 5.1 collective-permute-start
  96.6 52.5 %collective-permute-start.1 = (f32[512,1152]{1,0:T(8,128)S(1)}, f32[512,1152]{1,0:T(8,128)S(1)}, u32[]{:S(2)}, u32[]{:S(2)}) collective-permute-start(f32[512,1152]{1,0:T(8,128)S(1)} %add.82), channel_id=1, source_target_pairs={{0,32},{16,48},{32,0},{48,16},{64,96},{80,112},{96,64},{112,80},{1... | collective-permute-start | bytes 7077896 | tf_op jit(solution)/shard_map/ppermute | solution.py:94
  149.4 53.2 %collective-permute-start.2 = (f32[512,1152]{1,0:T(8,128)S(1)}, f32[512,1152]{1,0:T(8,128)S(1)}, u32[]{:S(2)}, u32[]{:S(2)}) collective-permute-start(f32[512,1152]{1,0:T(8,128)S(1)} %add.83), channel_id=1, source_target_pairs={{0,64},{16,80},{32,96},{48,112},{64,0},{80,16},{96,32},{112,48},{1... | collective-permute-start | bytes 7077896 | tf_op jit(solution)/shard_map/ppermute | solution.py:94
  203.8 108.5 %copy-start.8 = (f32[4608]{0:T(1024)S(1)}, f32[4608]{0:T(1024)}, u32[]{:S(2)}) copy-start(f32[4608]{0:T(1024)} %param.19) | copy-start | bytes 55300
  203.8 108.5 %all-gather.3.cloned.1.call-start = ((), (), s32[]{:S(2)}) async-start(), calls=%async_computation | async-start | bytes 5898240 | tf_op jit(solution)/shard_map/all_gather | solution.py:100
  204.5 290.0 %all-reduce.4.cloned.1.call-start = ((), (), s32[]{:S(2)}) async-start(), calls=%async_computation.2 | async-start | bytes 18874368 | tf_op jit(solution)/shard_map/psum | solution.py:114
  260.9 57.3 %copy-start.9 = (f32[4608]{0:T(1024)S(1)}, f32[4608]{0:T(1024)}, u32[]{:S(2)}) copy-start(f32[4608]{0:T(1024)} %param.23) | copy-start | bytes 55300
  260.9 57.3 %copy-start.12 = (f32[512]{0:T(512)S(1)}, f32[512]{0:T(512)}, u32[]{:S(2)}) copy-start(f32[512]{0:T(512)} %param.21) | copy-start | bytes 6148
  312.2 12.4 %slice-start = ((s8[4718592]{0:T(1024)(128)(4,1)}), s8[4194304]{0:T(1024)(128)(4,1)S(1)}, s32[]{:S(2)}) async-start(s8[4718592]{0:T(1024)(128)(4,1)} %bitcast.39), calls=%async_computation.4 | async-start | bytes 8388608
  318.2 6.4 %copy-start.2 = (bf16[512,4608]{1,0:T(8,128)(2,1)}, bf16[512,4608]{1,0:T(8,128)(2,1)S(1)}, u32[]{:S(2)}) copy-start(bf16[512,4608]{1,0:T(8,128)(2,1)S(1)} %fusion.3) | copy-start | bytes 14155780
  318.2 6.4 %slice-start.1 = ((s8[4718592]{0:T(1024)(128)(4,1)}), s8[524288]{0:T(1024)(128)(4,1)S(1)}, s32[]{:S(2)}) async-start(s8[4718592]{0:T(1024)(128)(4,1)} %bitcast.39), calls=%async_computation.5 | async-start | bytes 1048576
  502.9 6.7 %copy-start.4 = (bf16[512,4608]{1,0:T(8,128)(2,1)}, bf16[512,4608]{1,0:T(8,128)(2,1)S(1)}, u32[]{:S(2)}) copy-start(bf16[512,4608]{1,0:T(8,128)(2,1)S(1)} %get-tuple-element.7) | copy-start | bytes 14155780
  517.0 7.9 %copy-start.1 = (bf16[512,1152]{1,0:T(8,128)(2,1)S(1)}, bf16[512,1152]{1,0:T(8,128)(2,1)}, u32[]{:S(2)}) copy-start(bf16[512,1152]{1,0:T(8,128)(2,1)} %param.18) | copy-start | bytes 3538948
Sparse Core Ops, SparseCore 0:
  15.1 61.7 all-reduce.5
  203.9 53.5 all-gather.4
  259.2 52.9 all-gather.2
  329.9 164.6 all-reduce.3
